TPU v7x, 32 devices: a whole 2x2x4 slice. The times are simulated.
32 devices in a mesh: gx: 8 (over z, y), gy: 4 (over x, core).
Axes of the slice: x: 2, y: 2, z: 4, core: 2. Of those that a mesh axis runs over, the one named last changes fastest.
Arguments:
- layer_in: bfloat16 [8192, 2048], P('gx', 'gy'), may hold values from -15 to 15
- attn_gain: float32 [2048], replicated, may hold values from 0.25 to 1.75
- q_gain: float32 [128], replicated, may hold values from 0.5 to 5
- k_gain: float32 [128], replicated, may hold values from 0.5 to 5
- w_query: bfloat16 [2048, 2048], P('gx', 'gy'), may hold values from -0.125 to 0.125
- w_key: bfloat16 [2048, 1024], P('gx', 'gy'), may hold values from -0.125 to 0.125
- w_value: bfloat16 [2048, 1024], P('gx', 'gy'), may hold values from -0.125 to 0.125
- w_output: bfloat16 [2048, 2048], P('gy', 'gx'), may hold values from -0.375 to 0.375
- mlp_gain: float32 [2048], replicated, may hold values from 0.25 to 1.75
- w_gate: bfloat16 [2048, 6144], P('gx', 'gy'), may hold values from -0.125 to 0.125
- w_up: bfloat16 [2048, 6144], P('gx', 'gy'), may hold values from -0.125 to 0.125
- w_down: bfloat16 [6144, 2048], P('gy', 'gx'), may hold values from -0.078125 to 0.078125
- out_grad: bfloat16 [8192, 2048], P('gx', 'gy'), may hold values from -6 to 6
Outputs:
- layer_out: bfloat16 [8192, 2048], P('gx', 'gy')
- input_grad: float32 [8192, 2048], P('gx', 'gy')
- attn_gain_grad: float32 [2048], replicated
- q_gain_grad: float32 [128], replicated
- k_gain_grad: float32 [128], replicated
- query_grad: float32 [2048, 2048], P('gx', 'gy')
- key_grad: float32 [2048, 1024], P('gx', 'gy')
- value_grad: float32 [2048, 1024], P('gx', 'gy')
- output_grad: float32 [2048, 2048], P('gy', 'gx')
- mlp_gain_grad: float32 [2048], replicated
- gate_grad: float32 [2048, 6144], P('gx', 'gy')
- up_grad: float32 [2048, 6144], P('gx', 'gy')
- down_grad: float32 [6144, 2048], P('gy', 'gx')
All inputs are finite; a program needn't handle non-finite values.
Results may differ from a plain program's by a relative error of at most 0.02.
The roundings to bfloat16 on the way count: a program that leaves them out, or rounds other values in their place, can miss the bound.
Values may be sent and summed in bfloat16 or wider, within the bound.
No kernel may reach another device: no remote copies, remote signals or barrier semaphores. Data moves between devices by JAX's collectives and lax.ppermute only.
A program may use at most 256 MiB of HBM per device.

v0:
```python
import math
import jax
import jax.numpy as jnp
from jax import lax
from jax.sharding import PartitionSpec as P

D = 2048
HQ = 16
HK = 8
HD = 128
L = 512
epsilon = 1e-06
rope_base = 1000000.0


def rope_tables(length, dim_width):
    half_width = dim_width // 2
    frequency = rope_base ** (-(jnp.arange(half_width, dtype=jnp.float32) * (2.0 / dim_width)))
    angles = jnp.arange(length, dtype=jnp.float32)[:, None] * frequency[None, :]
    angles = jnp.concatenate([angles, angles], axis=1)
    return (jnp.cos(angles), jnp.sin(angles))


def rotate(tensor):
    half_width = tensor.shape[-1] // 2
    return jnp.concatenate([-tensor[..., half_width:], tensor[..., :half_width]], axis=-1)


def rotate_back(tensor):
    half_width = tensor.shape[-1] // 2
    return jnp.concatenate([tensor[..., half_width:], -tensor[..., :half_width]], axis=-1)


def head_norm(tensor, gain_vec):
    factor = lax.rsqrt(jnp.mean(tensor * tensor, axis=-1, keepdims=True) + epsilon)
    return (tensor * factor * gain_vec, factor)


def head_norm_back(upstream, tensor, factor, gain_vec):
    weighted = upstream * gain_vec
    return factor * weighted - tensor * factor**3 * jnp.mean(
        weighted * tensor, axis=-1, keepdims=True
    )


def matmul(left, right):
    return jnp.dot(left, right, preferred_element_type=jnp.float32)


def bein(form, left, right):
    return jnp.einsum(form, left, right, preferred_element_type=jnp.float32)


def causal_scores(query_rot, key_rot):
    inv_scale = 1.0 / math.sqrt(HD)
    scores = bein("sihgc,sjhc->shgij", query_rot, key_rot) * inv_scale
    causal = jnp.arange(L)[:, None] >= jnp.arange(L)[None, :]
    return jnp.where(causal, scores, -1e30)


def embed_share(share, column, total_width):
    return lax.dynamic_update_slice(jnp.zeros((total_width,), jnp.float32), share, (column,))


def on_device(
    layer_in,
    attn_gain,
    q_gain,
    k_gain,
    w_query,
    w_key,
    w_value,
    w_output,
    mlp_gain,
    w_gate,
    w_up,
    w_down,
    out_grad,
):
    row_count = layer_in.shape[0]
    part_width = layer_in.shape[1]
    seq_count = row_count // L
    group_size = HQ // HK
    inv_scale = 1.0 / math.sqrt(HD)
    column = lax.axis_index("gy") * part_width
    full_in, grad_full = (
        lax.all_gather(layer_in, "gy", axis=1, tiled=True),
        lax.all_gather(out_grad, "gy", axis=1, tiled=True),
    )
    in_float = full_in.astype(jnp.float32)
    scale_one = lax.rsqrt(jnp.mean(in_float * in_float, axis=1, keepdims=True) + epsilon)
    normed_one = (in_float * scale_one * attn_gain).astype(jnp.bfloat16)
    query_full, key_full, value_full, output_full = (
        lax.all_gather(w_query, "gx", axis=0, tiled=True),
        lax.all_gather(w_key, "gx", axis=0, tiled=True),
        lax.all_gather(w_value, "gx", axis=0, tiled=True),
        lax.all_gather(w_output, "gx", axis=1, tiled=True),
    )
    query_heads = query_full.shape[1] // HD
    key_heads = key_full.shape[1] // HD
    query_act = matmul(normed_one, query_full).reshape(row_count, query_heads, HD)
    key_act = matmul(normed_one, key_full).reshape(row_count, key_heads, HD)
    values = (
        matmul(normed_one, value_full).astype(jnp.bfloat16).reshape(seq_count, L, key_heads, HD)
    )
    query_normed, query_factor = head_norm(query_act, q_gain)
    key_normed, key_factor = head_norm(key_act, k_gain)
    cosine, sine = rope_tables(L, HD)
    cosine = cosine[None, :, None, :]
    sine = sine[None, :, None, :]
    query_seq = query_normed.reshape(seq_count, L, query_heads, HD)
    key_seq = key_normed.reshape(seq_count, L, key_heads, HD)
    query_rot = (
        (query_seq * cosine + rotate(query_seq) * sine)
        .astype(jnp.bfloat16)
        .reshape(seq_count, L, key_heads, group_size, HD)
    )
    key_rot = (key_seq * cosine + rotate(key_seq) * sine).astype(jnp.bfloat16)
    scores = causal_scores(query_rot, key_rot)
    row_top = jnp.max(scores, axis=-1, keepdims=True)
    log_total = row_top + jnp.log(jnp.sum(jnp.exp(scores - row_top), axis=-1, keepdims=True))
    probs = jnp.exp(scores - log_total).astype(jnp.bfloat16)
    attended = bein("shgij,sjhc->sihgc", probs, values).astype(jnp.bfloat16)
    attended_flat = attended.reshape(row_count, query_heads * HD)
    attn_sum = lax.psum(matmul(attended_flat, output_full), "gy")
    mid_float = in_float + attn_sum
    scale_two = lax.rsqrt(jnp.mean(mid_float * mid_float, axis=1, keepdims=True) + epsilon)
    normed_two = (mid_float * scale_two * mlp_gain).astype(jnp.bfloat16)
    gate_full, up_full, down_full = (
        lax.all_gather(w_gate, "gx", axis=0, tiled=True),
        lax.all_gather(w_up, "gx", axis=0, tiled=True),
        lax.all_gather(w_down, "gx", axis=1, tiled=True),
    )
    gate_act = matmul(normed_two, gate_full)
    up_act = matmul(normed_two, up_full)
    sigmoid_gate = jax.nn.sigmoid(gate_act)
    hidden = (gate_act * sigmoid_gate * up_act).astype(jnp.bfloat16)
    mlp_share = lax.psum_scatter(
        matmul(hidden, down_full).astype(jnp.bfloat16), "gy", scatter_dimension=1, tiled=True
    ).astype(jnp.float32)
    mid_share = lax.dynamic_slice_in_dim(mid_float, column, part_width, 1)
    layer_out = (mid_share + mlp_share).astype(jnp.bfloat16)
    grad_hidden = matmul(grad_full, down_full.T)
    down_term = matmul(hidden.T, grad_full)
    grad_gate = (
        grad_hidden * up_act * sigmoid_gate * (1.0 + gate_act * (1.0 - sigmoid_gate))
    ).astype(jnp.bfloat16)
    grad_up = (grad_hidden * gate_act * sigmoid_gate).astype(jnp.bfloat16)
    gate_term = matmul(normed_two.T, grad_gate)
    up_term = matmul(normed_two.T, grad_up)
    grad_two_part = matmul(grad_gate, gate_full.T) + matmul(grad_up, up_full.T)
    grad_two = lax.psum(grad_two_part, "gy")
    mlp_gain_all = jnp.sum(grad_two * mid_float * scale_two, axis=0)
    mlp_gain_own = lax.dynamic_slice_in_dim(mlp_gain_all, column, part_width, 0)
    grad_mid = (
        grad_full.astype(jnp.float32)
        + scale_two * mlp_gain * grad_two
        - mid_float
        * scale_two**3
        * jnp.mean(mlp_gain * grad_two * mid_float, axis=1, keepdims=True)
    )
    grad_mid_bf = grad_mid.astype(jnp.bfloat16)
    grad_mid_share = lax.dynamic_slice_in_dim(grad_mid, column, part_width, 1)
    gate_grad, up_grad, down_grad = (
        lax.psum_scatter(
            gate_term.astype(jnp.bfloat16), "gx", scatter_dimension=0, tiled=True
        ).astype(jnp.float32),
        lax.psum_scatter(
            up_term.astype(jnp.bfloat16), "gx", scatter_dimension=0, tiled=True
        ).astype(jnp.float32),
        lax.psum_scatter(
            down_term.astype(jnp.bfloat16), "gx", scatter_dimension=1, tiled=True
        ).astype(jnp.float32),
    )
    grad_att = matmul(grad_mid_bf, output_full.T).astype(jnp.bfloat16)
    output_term = matmul(attended_flat.T, grad_mid_bf)
    grad_att_seq = grad_att.reshape(seq_count, L, key_heads, group_size, HD)
    probs_again = jnp.exp(causal_scores(query_rot, key_rot) - log_total)
    probs_bf = probs_again.astype(jnp.bfloat16)
    delta = bein("sihgc,sihgc->shgi", grad_att_seq, attended)
    grad_probs = bein("sihgc,sjhc->shgij", grad_att_seq, values)
    grad_scores = (probs_again * (grad_probs - delta[..., None])).astype(jnp.bfloat16)
    grad_qrot = (bein("shgij,sjhc->sihgc", grad_scores, key_rot) * inv_scale).reshape(
        seq_count, L, query_heads, HD
    )
    grad_krot = bein("shgij,sihgc->sjhc", grad_scores, query_rot) * inv_scale
    grad_value_act = bein("shgij,sihgc->sjhc", probs_bf, grad_att_seq)
    grad_qn = (grad_qrot * cosine + rotate_back(grad_qrot * sine)).reshape(
        row_count, query_heads, HD
    )
    grad_kn = (grad_krot * cosine + rotate_back(grad_krot * sine)).reshape(row_count, key_heads, HD)
    q_gain_part = jnp.sum(grad_qn * query_act * query_factor, axis=(0, 1))
    k_gain_part = jnp.sum(grad_kn * key_act * key_factor, axis=(0, 1))
    grad_query = (
        head_norm_back(grad_qn, query_act, query_factor, q_gain)
        .astype(jnp.bfloat16)
        .reshape(row_count, query_heads * HD)
    )
    grad_key = (
        head_norm_back(grad_kn, key_act, key_factor, k_gain)
        .astype(jnp.bfloat16)
        .reshape(row_count, key_heads * HD)
    )
    grad_value = grad_value_act.astype(jnp.bfloat16).reshape(row_count, key_heads * HD)
    query_term = matmul(normed_one.T, grad_query)
    key_term = matmul(normed_one.T, grad_key)
    value_term = matmul(normed_one.T, grad_value)
    grad_one_part = (
        matmul(grad_query, query_full.T)
        + matmul(grad_key, key_full.T)
        + matmul(grad_value, value_full.T)
    )
    grad_one = lax.psum_scatter(
        grad_one_part.astype(jnp.bfloat16), "gy", scatter_dimension=1, tiled=True
    ).astype(jnp.float32)
    query_grad, key_grad, value_grad, output_grad = (
        lax.psum_scatter(
            query_term.astype(jnp.bfloat16), "gx", scatter_dimension=0, tiled=True
        ).astype(jnp.float32),
        lax.psum_scatter(
            key_term.astype(jnp.bfloat16), "gx", scatter_dimension=0, tiled=True
        ).astype(jnp.float32),
        lax.psum_scatter(
            value_term.astype(jnp.bfloat16), "gx", scatter_dimension=0, tiled=True
        ).astype(jnp.float32),
        lax.psum_scatter(
            output_term.astype(jnp.bfloat16), "gx", scatter_dimension=1, tiled=True
        ).astype(jnp.float32),
    )
    in_share = layer_in.astype(jnp.float32)
    gain_share = lax.dynamic_slice_in_dim(attn_gain, column, part_width, 0)
    row_stat = lax.psum(jnp.sum(gain_share * grad_one * in_share, axis=1, keepdims=True), "gy")
    input_grad = (
        grad_mid_share
        + scale_one * gain_share * grad_one
        - in_share * scale_one**3 * (row_stat / D)
    )
    attn_gain_own = jnp.sum(grad_one * in_share * scale_one, axis=0)
    attn_gain_grad, mlp_gain_grad, q_gain_grad, k_gain_grad = lax.psum(
        (
            embed_share(attn_gain_own, column, D),
            embed_share(mlp_gain_own, column, D),
            q_gain_part,
            k_gain_part,
        ),
        ("gx", "gy"),
    )
    return (
        layer_out,
        input_grad,
        attn_gain_grad,
        q_gain_grad,
        k_gain_grad,
        query_grad,
        key_grad,
        value_grad,
        output_grad,
        mlp_gain_grad,
        gate_grad,
        up_grad,
        down_grad,
    )


def solution(mesh):
    placed = (
        P("gx", "gy"),
        P(),
        P(),
        P(),
        P("gx", "gy"),
        P("gx", "gy"),
        P("gx", "gy"),
        P("gy", "gx"),
        P(),
        P("gx", "gy"),
        P("gx", "gy"),
        P("gy", "gx"),
        P("gx", "gy"),
    )
    return jax.shard_map(
        on_device,
        mesh=mesh,
        in_specs=placed,
        out_specs=(
            P("gx", "gy"),
            P("gx", "gy"),
            P(),
            P(),
            P(),
            P("gx", "gy"),
            P("gx", "gy"),
            P("gx", "gy"),
            P("gy", "gx"),
            P(),
            P("gx", "gy"),
            P("gx", "gy"),
            P("gy", "gx"),
        ),
        check_vma=False,
    )
```

profile of v0, /device:TPU:0, one launch (start us, length us, event | category | flops | bytes accessed | tf_op | source)
XLA Modules:
  0.0 1706.3 jit_solution(14412919391294357786)
XLA Ops:
  12.6 34.2 %all-gather.10.cloned.1.call-done = bf16[1024,2048]{1,0:T(8,128)(2,1)} async-done(((bf16[1024,512]{1,0:T(8,128)(2,1)}), bf16[1024,2048]{1,0:T(8,128)(2,1)}) %all-gather.10.cloned.1.call-update) | async-done | bytes 4194320 | tf_op jit(solution)/shard_map/all_gather | solution.py:87
  54.2 43.8 %all-gather.16.cloned.1.call-done = bf16[2048,512]{1,0:T(8,128)(2,1)} async-done(((bf16[256,512]{1,0:T(8,128)(2,1)}), bf16[2048,512]{1,0:T(8,128)(2,1)}) %all-gather.16.cloned.1.call-update) | async-done | bytes 2097168 | tf_op jit(solution)/shard_map/all_gather | solution.py:94
  98.0 5.3 multiply_reduce_fusion.5
  109.0 30.0 %all-gather.14.cloned.1.call-done = bf16[2048,256]{1,0:T(8,128)(2,1)} async-done(((bf16[256,256]{1,0:T(8,128)(2,1)}), bf16[2048,256]{1,0:T(8,128)(2,1)}) %all-gather.14.cloned.1.call-update) | async-done | bytes 1048592 | tf_op jit(solution)/shard_map/all_gather | solution.py:95
  139.0 3.8 multiply_reduce_fusion.7
  144.4 35.6 %all-gather.12.cloned.1.call-done = bf16[2048,256]{1,0:T(8,128)(2,1)} async-done(((bf16[256,256]{1,0:T(8,128)(2,1)}), bf16[2048,256]{1,0:T(8,128)(2,1)}) %all-gather.12.cloned.1.call-update) | async-done | bytes 1048592 | tf_op jit(solution)/shard_map/all_gather | solution.py:96
  180.0 3.7 convolution_convert_fusion.9
  200.9 30.0 %all-gather.18.cloned.1.call-done = bf16[512,2048]{1,0:T(8,128)(2,1)} async-done(((bf16[512,256]{1,0:T(8,128)(2,1)}), bf16[512,2048]{1,0:T(8,128)(2,1)}) %all-gather.18.cloned.1.call-update) | async-done | bytes 2097168 | tf_op jit(solution)/shard_map/all_gather | solution.py:97
  230.9 7.5 fusion.48
  241.4 148.3 %all-reduce.4.cloned.1.call-done = f32[1024,2048]{1,0:T(8,128)} async-done(((f32[1024,2048]{1,0:T(8,128)}), f32[1024,2048]{1,0:T(8,128)}) %all-reduce.4.cloned.1.call-update) | async-done | bytes 8388624 | tf_op jit(solution)/shard_map/psum | solution.py:125
  389.7 5.7 multiply_reduce_fusion.2
  401.6 89.2 %all-gather.20.cloned.1.call-done = bf16[2048,1536]{1,0:T(8,128)(2,1)} async-done(((bf16[256,1536]{1,0:T(8,128)(2,1)}), bf16[2048,1536]{1,0:T(8,128)(2,1)}) %all-gather.20.cloned.1.call-update) | async-done | bytes 6291472 | tf_op jit(solution)/shard_map/all_gather | solution.py:130
  490.7 11.7 fusion.49
  502.4 87.4 %all-gather.22.cloned.1.call-done = bf16[2048,1536]{1,0:T(8,128)(2,1)} async-done(((bf16[256,1536]{1,0:T(8,128)(2,1)}), bf16[2048,1536]{1,0:T(8,128)(2,1)}) %all-gather.22.cloned.1.call-update) | async-done | bytes 6291472 | tf_op jit(solution)/shard_map/all_gather | solution.py:131
  589.8 11.8 fusion.50
  601.6 22.5 %all-gather.26.cloned.1.call-done = bf16[1024,2048]{1,0:T(8,128)(2,1)} async-done(((bf16[1024,512]{1,0:T(8,128)(2,1)}), bf16[1024,2048]{1,0:T(8,128)(2,1)}) %all-gather.26.cloned.1.call-update) | async-done | bytes 4194320 | tf_op jit(solution)/shard_map/all_gather | solution.py:88
  624.1 101.4 %all-gather.24.cloned.1.call-done = bf16[1536,2048]{1,0:T(8,128)(2,1)} async-done(((bf16[1536,256]{1,0:T(8,128)(2,1)}), bf16[1536,2048]{1,0:T(8,128)(2,1)}) %all-gather.24.cloned.1.call-update) | async-done | bytes 6291472 | tf_op jit(solution)/shard_map/all_gather | solution.py:132
  725.5 16.4 multiply_convert_fusion.1
  741.9 10.0 fusion.51
  751.9 10.7 convolution_add_fusion
  764.0 149.8 %all-reduce.6.cloned.1.call-done = f32[1024,2048]{1,0:T(8,128)} async-done(((f32[1024,2048]{1,0:T(8,128)}), f32[1024,2048]{1,0:T(8,128)}) %all-reduce.6.cloned.1.call-update) | async-done | bytes 8388624 | tf_op jit(solution)/shard_map/psum | solution.py:152
  913.8 7.2 multiply_reduce_fusion
  923.3 4.6 multiply_subtract_fusion
  931.1 4.9 fusion.24
  941.9 6.8 fusion.28
  950.9 4.1 copy.171
  957.0 4.6 convolution_convert_fusion.6
  961.9 6.5 fusion.4
  977.6 11.0 convolution_convert_fusion.3
  992.5 4.3 convolution_multiply_fusion
  999.8 4.7 copy.145
  1012.7 5.9 multiply_reduce_fusion.4
  1026.1 3.8 convolution_convert_fusion.5
  1030.0 7.2 convolution_convert_fusion.4
  1045.1 11.5 convolution_convert_fusion.2
  1056.8 11.5 convolution_convert_fusion.1
  1068.4 11.3 convolution_convert_fusion
  1082.4 11.0 reduce-scatter.16.cloned.1.call-done
  1095.0 44.2 %reduce-scatter.10.cloned.1.call-done = bf16[1024,512]{1,0:T(8,128)(2,1)} async-done(((bf16[1024,2048]{1,0:T(8,128)(2,1)}), bf16[1024,512]{1,0:T(8,128)(2,1)}) %reduce-scatter.10.cloned.1.call-update) | async-done | bytes 1048592 | tf_op jit(solution)/shard_map/reduce_scatter | solution.py:138
  1142.4 69.1 %reduce-scatter.14.cloned.1.call-done = bf16[256,512]{1,0:T(8,128)(2,1)} async-done(((bf16[2048,512]{1,0:T(8,128)(2,1)}), bf16[256,512]{1,0:T(8,128)(2,1)}) %reduce-scatter.14.cloned.1.call-update) | async-done | bytes 262160 | tf_op jit(solution)/shard_map/reduce_scatter | solution.py:217
  1213.3 69.6 %reduce-scatter.20.cloned.1.call-done = bf16[512,256]{1,0:T(8,128)(2,1)} async-done(((bf16[512,2048]{1,0:T(8,128)(2,1)}), bf16[512,256]{1,0:T(8,128)(2,1)}) %reduce-scatter.20.cloned.1.call-update) | async-done | bytes 262160 | tf_op jit(solution)/shard_map/reduce_scatter | solution.py:226
  1284.7 43.9 %reduce-scatter.12.cloned.1.call-done = bf16[1024,512]{1,0:T(8,128)(2,1)} async-done(((bf16[1024,2048]{1,0:T(8,128)(2,1)}), bf16[1024,512]{1,0:T(8,128)(2,1)}) %reduce-scatter.12.cloned.1.call-update) | async-done | bytes 1048592 | tf_op jit(solution)/shard_map/reduce_scatter | solution.py:213
  1331.2 118.9 %reduce-scatter.22.cloned.1.call-done = bf16[256,1536]{1,0:T(8,128)(2,1)} async-done(((bf16[2048,1536]{1,0:T(8,128)(2,1)}), bf16[256,1536]{1,0:T(8,128)(2,1)}) %reduce-scatter.22.cloned.1.call-update) | async-done | bytes 786448 | tf_op jit(solution)/shard_map/reduce_scatter | solution.py:165
  1452.6 118.4 %reduce-scatter.24.cloned.1.call-done = bf16[256,1536]{1,0:T(8,128)(2,1)} async-done(((bf16[2048,1536]{1,0:T(8,128)(2,1)}), bf16[256,1536]{1,0:T(8,128)(2,1)}) %reduce-scatter.24.cloned.1.call-update) | async-done | bytes 786448 | tf_op jit(solution)/shard_map/reduce_scatter | solution.py:168
  1573.5 43.1 %all-reduce = (f32[2048]{0:T(1024)}, f32[128]{0:T(128)}, f32[128]{0:T(128)}, f32[2048]{0:T(1024)}) all-reduce(f32[2048]{0:T(1024)S(1)} %dynamic_update_slice.6, f32[128]{0:T(128)S(1)} %bitcast_reduce_fusion, f32[128]{0:T(128)S(1)} %get-tuple-element.21, ...), channel_id=1, replica_groups=mesh['gx'=8,'gy'=4] {'gx','gy'}, use_global_device_ids=true, to_apply=%region_16.17 | all-reduce | flops 4352 | bytes 34816 | tf_op jit(solution)/shard_map/psum | solution.py:239
  1616.6 6.6 psum.51
  1623.1 70.1 %reduce-scatter.26.cloned.1.call-done = bf16[1536,256]{1,0:T(8,128)(2,1)} async-done(((bf16[1536,2048]{1,0:T(8,128)(2,1)}), bf16[1536,256]{1,0:T(8,128)(2,1)}) %reduce-scatter.26.cloned.1.call-update) | async-done | bytes 786448 | tf_op jit(solution)/shard_map/reduce_scatter | solution.py:171
  1695.7 3.5 fusion.8
  (233 shorter events, 123.7 us)
Async XLA Ops:
  7.2 44.0 %copy-start.48 = (f32[2048]{0:T(1024)S(1)}, f32[2048]{0:T(1024)}, u32[]{:S(2)}) copy-start(f32[2048]{0:T(1024)} %param.14) | copy-start | bytes 24580
  7.2 39.6 %all-gather.10.cloned.1.call-start = ((), (), s32[]{:S(2)}) async-start(), calls=%async_computation.9 | async-start | bytes 5242880 | tf_op jit(solution)/shard_map/all_gather | solution.py:87
  7.9 90.1 %all-gather.16.cloned.1.call-start = ((), (), s32[]{:S(2)}) async-start(), calls=%async_computation.12 | async-start | bytes 2359296 | tf_op jit(solution)/shard_map/all_gather | solution.py:94
  8.7 130.3 %all-gather.14.cloned.1.call-start = ((), (), s32[]{:S(2)}) async-start(), calls=%async_computation.11 | async-start | bytes 1179648 | tf_op jit(solution)/shard_map/all_gather | solution.py:95
  9.4 170.6 %all-gather.12.cloned.1.call-start = ((), (), s32[]{:S(2)}) async-start(), calls=%async_computation.10 | async-start | bytes 1179648 | tf_op jit(solution)/shard_map/all_gather | solution.py:96
  10.0 221.0 %all-gather.18.cloned.1.call-start = ((), (), s32[]{:S(2)}) async-start(), calls=%async_computation.13 | async-start | bytes 2359296 | tf_op jit(solution)/shard_map/all_gather | solution.py:97
  10.6 379.1 %all-reduce.4.cloned.1.call-start = ((), (), s32[]{:S(2)}) async-start(), calls=%async_computation.14 | async-start | bytes 16777216 | tf_op jit(solution)/shard_map/psum | solution.py:125
  46.8 4.4 copy-start.2
  103.3 5.7 copy-start.4
  144.3 41.8 %copy-start.41 = (f32[1024,4]{0,1:T(4,128)}, f32[1024,4]{0,1:T(4,128)S(1)}, u32[]{:S(2)}) copy-start(f32[1024,4]{0,1:T(4,128)S(1)} %get-tuple-element.45) | copy-start | bytes 49156
  144.4 40.3 %copy-start.51 = (f32[128]{0:T(128)S(1)}, f32[128]{0:T(128)}, u32[]{:S(2)}) copy-start(f32[128]{0:T(128)} %param.16) | copy-start | bytes 1540
  196.2 42.3 %copy-start.19 = (bf16[2,2,128,2,512]{4,2,3,1,0:T(8,128)(2,1)}, bf16[2,2,128,2,512]{4,2,3,1,0:T(8,128)(2,1)S(1)}, u32[]{:S(2)}) copy-start(bf16[2,2,128,2,512]{4,2,3,1,0:T(8,128)(2,1)S(1)} %convolution_convert_fusion.8) | copy-start | bytes 3145732
  238.5 252.3 %all-gather.20.cloned.1.call-start = ((), (), s32[]{:S(2)}) async-start(), calls=%async_computation.15 | async-start | bytes 7077888 | tf_op jit(solution)/shard_map/all_gather | solution.py:130
  239.2 350.6 %all-gather.22.cloned.1.call-start = ((), (), s32[]{:S(2)}) async-start(), calls=%async_computation.16 | async-start | bytes 7077888 | tf_op jit(solution)/shard_map/all_gather | solution.py:131
  240.0 384.1 %all-gather.26.cloned.1.call-start = ((), (), s32[]{:S(2)}) async-start(), calls=%async_computation.19 | async-start | bytes 5242880 | tf_op jit(solution)/shard_map/all_gather | solution.py:88
  240.7 484.8 %all-gather.24.cloned.1.call-start = ((), (), s32[]{:S(2)}) async-start(), calls=%async_computation.17 | async-start | bytes 7077888 | tf_op jit(solution)/shard_map/all_gather | solution.py:132
  241.3 157.4 %copy-start.43 = (f32[2048]{0:T(1024)S(1)}, f32[2048]{0:T(1024)}, u32[]{:S(2)}) copy-start(f32[2048]{0:T(1024)} %param.21) | copy-start | bytes 24580
  241.3 672.5 %all-reduce.6.cloned.1.call-start = ((), (), s32[]{:S(2)}) async-start(), calls=%async_computation.20 | async-start | bytes 16777216 | tf_op jit(solution)/shard_map/psum | solution.py:152
  395.4 3.3 copy-start
  741.9 10.0 copy-start.54
  741.9 10.0 copy-start.52
  762.6 318.1 %reduce-scatter.18.cloned.1.call-start = ((), (), s32[]{:S(2)}) async-start(), calls=%async_computation.24 | async-start | bytes 1179648 | tf_op jit(solution)/shard_map/reduce_scatter | solution.py:223
  913.8 8.2 copy-start.3
  913.8 9.4 copy-start.18
  948.8 6.2 copy-start.20
  961.6 6.8 copy-start.11
  961.6 131.8 %reduce-scatter.16.cloned.1.call-start = ((), (), s32[]{:S(2)}) async-start(), calls=%async_computation.23 | async-start | bytes 1179648 | tf_op jit(solution)/shard_map/reduce_scatter | solution.py:220
  961.9 6.6 copy-start.15
  977.5 161.7 %reduce-scatter.10.cloned.1.call-start = ((), (), s32[]{:S(2)}) async-start(), calls=%async_computation.18 | async-start | bytes 5242880 | tf_op jit(solution)/shard_map/reduce_scatter | solution.py:138
  988.6 3.9 copy-start.17
  988.6 222.9 %reduce-scatter.14.cloned.1.call-start = ((), (), s32[]{:S(2)}) async-start(), calls=%async_computation.22 | async-start | bytes 2359296 | tf_op jit(solution)/shard_map/reduce_scatter | solution.py:217
  996.8 7.7 copy-start.27
  999.8 4.7 copy-start.7
  1018.5 5.3 copy-start.34
  1018.6 5.3 copy-start.42
  1018.6 5.3 copy-start.44
  1026.1 3.9 copy-start.30
  1029.9 7.6 copy-start.32
  1029.9 7.6 copy-start.35
  1029.9 253.0 %reduce-scatter.20.cloned.1.call-start = ((), (), s32[]{:S(2)}) async-start(), calls=%async_computation.25 | async-start | bytes 2359296 | tf_op jit(solution)/shard_map/reduce_scatter | solution.py:226
  1037.3 291.4 %reduce-scatter.12.cloned.1.call-start = ((), (), s32[]{:S(2)}) async-start(), calls=%async_computation.21 | async-start | bytes 5242880 | tf_op jit(solution)/shard_map/reduce_scatter | solution.py:213
  1045.0 405.1 %reduce-scatter.22.cloned.1.call-start = ((), (), s32[]{:S(2)}) async-start(), calls=%async_computation.26 | async-start | bytes 7077888 | tf_op jit(solution)/shard_map/reduce_scatter | solution.py:165
  1056.6 514.5 %reduce-scatter.24.cloned.1.call-start = ((), (), s32[]{:S(2)}) async-start(), calls=%async_computation.27 | async-start | bytes 7077888 | tf_op jit(solution)/shard_map/reduce_scatter | solution.py:168
  1068.3 625.0 %reduce-scatter.26.cloned.1.call-start = ((), (), s32[]{:S(2)}) async-start(), calls=%async_computation.28 | async-start | bytes 7077888 | tf_op jit(solution)/shard_map/reduce_scatter | solution.py:171
  1079.7 249.0 %copy-start.9 = (bf16[1024,512]{1,0:T(8,128)(2,1)S(1)}, bf16[1024,512]{1,0:T(8,128)(2,1)}, u32[]{:S(2)}) copy-start(bf16[1024,512]{1,0:T(8,128)(2,1)} %param.13) | copy-start | bytes 3145732
  1079.7 249.0 %copy-start.46 = (f32[1024]{0:T(1024)S(1)}, f32[1024]{0:T(1024)}, u32[]{:S(2)}) copy-start(f32[1024]{0:T(1024)} %copy-done.45) | copy-start | bytes 12292
  1284.7 411.0 %copy-start.47 = (f32[1024]{0:T(1024)S(1)}, f32[1024]{0:T(1024)}, u32[]{:S(2)}) copy-start(f32[1024]{0:T(1024)} %get-tuple-element.48) | copy-start | bytes 12292
  1328.7 367.0 %copy-start.25 = (bf16[1024,512]{1,0:T(8,128)(2,1)S(1)}, bf16[1024,512]{1,0:T(8,128)(2,1)}, u32[]{:S(2)}) copy-start(bf16[1024,512]{1,0:T(8,128)(2,1)} %reduce-scatter.12.cloned.1.call-done) | copy-start | bytes 3145732
  (28 other events, 55.1 us)
Sparse Core Ops, SparseCore 0:
  9.6 37.1 all-gather.9
  48.9 49.0 all-gather.15
  100.1 38.7 all-gather.13
  141.0 38.9 all-gather.11
  181.9 49.0 all-gather.17
  238.6 151.0 all-reduce.3
  391.9 98.8 all-gather.19
  492.9 96.8 all-gather.21
  591.4 32.6 all-gather.25
  626.0 99.4 all-gather.23
  762.8 151.0 all-reduce.5
  961.7 64.4 reduce-scatter.17
  1030.2 63.1 reduce-scatter.15
  1095.7 43.3 reduce-scatter.9
  1143.1 68.3 reduce-scatter.13
  1214.9 67.9 reduce-scatter.19
  1285.3 43.2 reduce-scatter.11
  1332.1 118.0 reduce-scatter.21
  1453.7 117.2 reduce-scatter.23
  1574.5 118.7 reduce-scatter.25
where the time goes:
time: 1710 us
  waiting for transfers between devices  1320 us (77%)
  matrix products  179 us (10%)
  other arithmetic  71 us (4%)
  local copies, waits for them, and re-layouts  65.8 us (4%)
  blocking collectives  49.6 us (3%)
    dot_general x21, matrix products, matmul(): return jnp.dot(left, right, preferred_element_type=jnp.float32)  156 us
    psum x1, waiting for transfers between devices, on_device(): grad_two = lax.psum(grad_two_part, 'gy')  150 us
    psum x1, waiting for transfers between devices, on_device(): attn_sum = lax.psum(matmul(attended_flat, output_full), 'gy')  148 us
    reduce_scatter x1, waiting for transfers between devices, on_device(): lax.psum_scatter(gate_term.astype(jnp.bfloat16), 'gx', scatter_dimension=...  119 us
    reduce_scatter x1, waiting for transfers between devices, on_device(): lax.psum_scatter(up_term.astype(jnp.bfloat16), 'gx', scatter_dimension=0,...  118 us
    all_gather x1, waiting for transfers between devices, on_device(): lax.all_gather(w_down, 'gx', axis=1, tiled=True)  101 us
    all_gather x1, waiting for transfers between devices, on_device(): lax.all_gather(w_gate, 'gx', axis=0, tiled=True)  89.2 us
    all_gather x1, waiting for transfers between devices, on_device(): lax.all_gather(w_up, 'gx', axis=0, tiled=True)  87.4 us
  transfers between devices with their start and end apart: 20, of which 19 were waited for; matrix products, arithmetic and copies ran while one was open for 12% of the time, Pallas kernels for 0%

commit v1 on v0

--- a/solution.py
+++ b/solution.py
@@ -11,6 +11,24 @@
 L = 512
 epsilon = 1e-06
 rope_base = 1000000.0
+
+
+def ring_gather(value, axis, dim):
+    ways, here, step = (lax.axis_size(axis), lax.axis_index(axis), value.shape[dim])
+    lengths = [n * ways if d == dim else n for d, n in enumerate(value.shape)]
+    full = lax.dynamic_update_slice_in_dim(
+        jnp.zeros(lengths, value.dtype), value, here * step, axis=dim
+    )
+    going_up = going_down = value
+    for far in range(1, ways // 2 + 1):
+        going_up = lax.ppermute(going_up, axis, [(d, (d + 1) % ways) for d in range(ways)])
+        full = lax.dynamic_update_slice_in_dim(full, going_up, (here - far) % ways * step, axis=dim)
+        if 2 * far < ways:
+            going_down = lax.ppermute(going_down, axis, [(d, (d - 1) % ways) for d in range(ways)])
+            full = lax.dynamic_update_slice_in_dim(
+                full, going_down, (here + far) % ways * step, axis=dim
+            )
+    return full
 
 
 def rope_tables(length, dim_width):
@@ -127,7 +145,7 @@
     scale_two = lax.rsqrt(jnp.mean(mid_float * mid_float, axis=1, keepdims=True) + epsilon)
     normed_two = (mid_float * scale_two * mlp_gain).astype(jnp.bfloat16)
     gate_full, up_full, down_full = (
-        lax.all_gather(w_gate, "gx", axis=0, tiled=True),
+        ring_gather(w_gate, "gx", 0),
         lax.all_gather(w_up, "gx", axis=0, tiled=True),
         lax.all_gather(w_down, "gx", axis=1, tiled=True),
     )

time: 1710 us -> 1620 us (0.947)
  waiting for transfers between devices: 1320 us -> 1180 us
  starting transfers between devices: 1.8 us -> 43.7 us
    psum x1, waiting for transfers between devices: 148 us -> 22.3 us  [on_device(): attn_sum = lax.psum(matmul(attended_flat, output_full), 'gy')]
    all_gather x1 -> x0, waiting for transfers between devices: 89.2 us -> none  [on_device(): lax.all_gather(w_gate, 'gx', axis=0, tiled=True)]
    ppermute x0 -> x7, waiting for transfers between devices: none -> 69.4 us  [the longest x4 69.4 us: ring_gather(): lax.ppermute(going_up, axis, [(d, (d + 1) % ways) for d in range(ways)])]
    ppermute x0 -> x7, starting transfers between devices: none -> 41.9 us  [the longest x3 32.8 us: ring_gather(): lax.ppermute(going_down, axis, [(d, (d - 1) % ways) for d in range(ways)])]
  transfers between devices with their start and end apart: 20 -> 26, of which waited for: 19 -> 22; matrix products, arithmetic and copies ran while one was open for 12% -> 13% of each run, Pallas kernels for 0% -> 0%
where the time goes in v1:
time: 1620 us
  waiting for transfers between devices  1180 us (73%)
  matrix products  177 us (11%)
  local copies, waits for them, and re-layouts  81.4 us (5%)
  other arithmetic  71.8 us (4%)
  blocking collectives  49.6 us (3%)
  starting transfers between devices  43.7 us (3%)
    dot_general x21, matrix products, matmul(): return jnp.dot(left, right, preferred_element_type=jnp.float32)  154 us
    psum x1, waiting for transfers between devices, on_device(): grad_two = lax.psum(grad_two_part, 'gy')  150 us
    reduce_scatter x1, waiting for transfers between devices, on_device(): lax.psum_scatter(gate_term.astype(jnp.bfloat16), 'gx', scatter_dimension=...  119 us
    reduce_scatter x1, waiting for transfers between devices, on_device(): lax.psum_scatter(up_term.astype(jnp.bfloat16), 'gx', scatter_dimension=0,...  118 us
    all_gather x1, waiting for transfers between devices, on_device(): lax.all_gather(w_down, 'gx', axis=1, tiled=True)  102 us
    all_gather x1, waiting for transfers between devices, on_device(): lax.all_gather(w_up, 'gx', axis=0, tiled=True)  89.3 us
    reduce_scatter x1, waiting for transfers between devices, on_device(): lax.psum_scatter(down_term.astype(jnp.bfloat16), 'gx', scatter_dimension=...  70.3 us
    reduce_scatter x1, waiting for transfers between devices, on_device(): lax.psum_scatter(query_term.astype(jnp.bfloat16), 'gx', scatter_dimension...  69.6 us
  transfers between devices with their start and end apart: 26, of which 22 were waited for; matrix products, arithmetic and copies ran while one was open for 13% of the time, Pallas kernels for 0%

profile of v1, /device:TPU:0, one launch (start us, length us, event | category | flops | bytes accessed | tf_op | source)
XLA Modules:
  0.0 1616.5 jit_solution(7528630260785945360)
XLA Ops:
  12.6 34.2 %all-gather.9.cloned.1.call-done = bf16[1024,2048]{1,0:T(8,128)(2,1)} async-done(((bf16[1024,512]{1,0:T(8,128)(2,1)}), bf16[1024,2048]{1,0:T(8,128)(2,1)}) %all-gather.9.cloned.1.call-update) | async-done | bytes 4194320 | tf_op jit(solution)/shard_map/all_gather | solution.py:105
  54.3 43.7 %all-gather.15.cloned.1.call-done = bf16[2048,512]{1,0:T(8,128)(2,1)} async-done(((bf16[256,512]{1,0:T(8,128)(2,1)}), bf16[2048,512]{1,0:T(8,128)(2,1)}) %all-gather.15.cloned.1.call-update) | async-done | bytes 2097168 | tf_op jit(solution)/shard_map/all_gather | solution.py:112
  98.0 5.3 multiply_reduce_fusion.5
  109.1 29.9 %all-gather.13.cloned.1.call-done = bf16[2048,256]{1,0:T(8,128)(2,1)} async-done(((bf16[256,256]{1,0:T(8,128)(2,1)}), bf16[2048,256]{1,0:T(8,128)(2,1)}) %all-gather.13.cloned.1.call-update) | async-done | bytes 1048592 | tf_op jit(solution)/shard_map/all_gather | solution.py:113
  145.0 35.0 %all-gather.11.cloned.1.call-done = bf16[2048,256]{1,0:T(8,128)(2,1)} async-done(((bf16[256,256]{1,0:T(8,128)(2,1)}), bf16[2048,256]{1,0:T(8,128)(2,1)}) %all-gather.11.cloned.1.call-update) | async-done | bytes 1048592 | tf_op jit(solution)/shard_map/all_gather | solution.py:114
  200.9 30.1 %all-gather.17.cloned.1.call-done = bf16[512,2048]{1,0:T(8,128)(2,1)} async-done(((bf16[512,256]{1,0:T(8,128)(2,1)}), bf16[512,2048]{1,0:T(8,128)(2,1)}) %all-gather.17.cloned.1.call-update) | async-done | bytes 2097168 | tf_op jit(solution)/shard_map/all_gather | solution.py:115
  231.0 7.6 fusion.48
  245.6 30.5 %collective-permute-done = bf16[256,1536]{1,0:T(8,128)(2,1)S(1)} collective-permute-done((bf16[256,1536]{1,0:T(8,128)(2,1)S(1)}, bf16[256,1536]{1,0:T(8,128)(2,1)S(1)}, u32[]{:S(2)}, u32[]{:S(2)}) %collective-permute-start) | collective-permute-done | bytes 786464 | tf_op jit(solution)/shard_map/ppermute | solution.py:24
  278.6 16.7 %collective-permute-start.3 = (bf16[256,1536]{1,0:T(8,128)(2,1)}, bf16[256,1536]{1,0:T(8,128)(2,1)}, u32[]{:S(2)}, u32[]{:S(2)}) collective-permute-start(bf16[256,1536]{1,0:T(8,128)(2,1)} %collective-permute-done.1), channel_id=1, source_target_pairs={{0,28},{4,0},{8,4},{12,8},{16,12},{20,16},{24,20},{28,24},{1,29},{... | collective-permute-start | bytes 2359304 | tf_op jit(solution)/shard_map/ppermute | solution.py:27
  295.3 16.3 %collective-permute-done.2 = bf16[256,1536]{1,0:T(8,128)(2,1)} collective-permute-done((bf16[256,1536]{1,0:T(8,128)(2,1)S(1)}, bf16[256,1536]{1,0:T(8,128)(2,1)}, u32[]{:S(2)}, u32[]{:S(2)}) %collective-permute-start.2) | collective-permute-done | bytes 786464 | tf_op jit(solution)/shard_map/ppermute | solution.py:24
  319.2 12.9 collective-permute-start.5
  334.1 12.6 collective-permute-done.4
  356.5 10.0 collective-permute-done.6
  367.5 22.3 %all-reduce.4.cloned.1.call-done = f32[1024,2048]{1,0:T(8,128)} async-done(((f32[1024,2048]{1,0:T(8,128)}), f32[1024,2048]{1,0:T(8,128)}) %all-reduce.4.cloned.1.call-update) | async-done | bytes 8388624 | tf_op jit(solution)/shard_map/psum | solution.py:143
  389.8 5.7 multiply_reduce_fusion.2
  401.5 89.3 %all-gather.19.cloned.1.call-done = bf16[2048,1536]{1,0:T(8,128)(2,1)} async-done(((bf16[256,1536]{1,0:T(8,128)(2,1)}), bf16[2048,1536]{1,0:T(8,128)(2,1)}) %all-gather.19.cloned.1.call-update) | async-done | bytes 6291472 | tf_op jit(solution)/shard_map/all_gather | solution.py:149
  490.8 11.7 fusion.49
  502.5 22.5 %all-gather.23.cloned.1.call-done = bf16[1024,2048]{1,0:T(8,128)(2,1)} async-done(((bf16[1024,512]{1,0:T(8,128)(2,1)}), bf16[1024,2048]{1,0:T(8,128)(2,1)}) %all-gather.23.cloned.1.call-update) | async-done | bytes 4194320 | tf_op jit(solution)/shard_map/all_gather | solution.py:106
  525.1 101.6 %all-gather.21.cloned.1.call-done = bf16[1536,2048]{1,0:T(8,128)(2,1)} async-done(((bf16[1536,256]{1,0:T(8,128)(2,1)}), bf16[1536,2048]{1,0:T(8,128)(2,1)}) %all-gather.21.cloned.1.call-update) | async-done | bytes 6291472 | tf_op jit(solution)/shard_map/all_gather | solution.py:150
  626.6 11.9 fusion.50
  638.5 15.9 multiply_convert_fusion.2
  654.4 6.7 fusion.51
  661.1 11.9 convolution_add_fusion
  674.4 149.8 %all-reduce.6.cloned.1.call-done = f32[1024,2048]{1,0:T(8,128)} async-done(((f32[1024,2048]{1,0:T(8,128)}), f32[1024,2048]{1,0:T(8,128)}) %all-reduce.6.cloned.1.call-update) | async-done | bytes 8388624 | tf_op jit(solution)/shard_map/psum | solution.py:170
  824.2 7.4 multiply_reduce_fusion
  833.6 4.6 multiply_subtract_fusion
  841.5 4.9 fusion.24
  852.3 6.8 fusion.28
  867.3 4.6 convolution_convert_fusion.6
  872.5 6.5 fusion.4
  888.0 11.0 convolution_convert_fusion.3
  900.2 7.2 convolution_convert_fusion.4
  910.8 4.2 convolution_multiply_fusion
  918.0 4.7 copy.145
  930.9 5.9 multiply_reduce_fusion.4
  955.8 11.5 convolution_convert_fusion.2
  967.7 11.5 convolution_convert_fusion.1
  979.3 11.3 convolution_convert_fusion
  993.3 10.2 reduce-scatter.16.cloned.1.call-done
  1005.1 44.4 %reduce-scatter.10.cloned.1.call-done = bf16[1024,512]{1,0:T(8,128)(2,1)} async-done(((bf16[1024,2048]{1,0:T(8,128)(2,1)}), bf16[1024,512]{1,0:T(8,128)(2,1)}) %reduce-scatter.10.cloned.1.call-update) | async-done | bytes 1048592 | tf_op jit(solution)/shard_map/reduce_scatter | solution.py:156
  1052.7 69.1 %reduce-scatter.20.cloned.1.call-done = bf16[512,256]{1,0:T(8,128)(2,1)} async-done(((bf16[512,2048]{1,0:T(8,128)(2,1)}), bf16[512,256]{1,0:T(8,128)(2,1)}) %reduce-scatter.20.cloned.1.call-update) | async-done | bytes 262160 | tf_op jit(solution)/shard_map/reduce_scatter | solution.py:244
  1123.6 69.6 %reduce-scatter.14.cloned.1.call-done = bf16[256,512]{1,0:T(8,128)(2,1)} async-done(((bf16[2048,512]{1,0:T(8,128)(2,1)}), bf16[256,512]{1,0:T(8,128)(2,1)}) %reduce-scatter.14.cloned.1.call-update) | async-done | bytes 262160 | tf_op jit(solution)/shard_map/reduce_scatter | solution.py:235
  1195.1 44.0 %reduce-scatter.12.cloned.1.call-done = bf16[1024,512]{1,0:T(8,128)(2,1)} async-done(((bf16[1024,2048]{1,0:T(8,128)(2,1)}), bf16[1024,512]{1,0:T(8,128)(2,1)}) %reduce-scatter.12.cloned.1.call-update) | async-done | bytes 1048592 | tf_op jit(solution)/shard_map/reduce_scatter | solution.py:231
  1241.6 118.9 %reduce-scatter.22.cloned.1.call-done = bf16[256,1536]{1,0:T(8,128)(2,1)} async-done(((bf16[2048,1536]{1,0:T(8,128)(2,1)}), bf16[256,1536]{1,0:T(8,128)(2,1)}) %reduce-scatter.22.cloned.1.call-update) | async-done | bytes 786448 | tf_op jit(solution)/shard_map/reduce_scatter | solution.py:183
  1362.9 118.3 %reduce-scatter.24.cloned.1.call-done = bf16[256,1536]{1,0:T(8,128)(2,1)} async-done(((bf16[2048,1536]{1,0:T(8,128)(2,1)}), bf16[256,1536]{1,0:T(8,128)(2,1)}) %reduce-scatter.24.cloned.1.call-update) | async-done | bytes 786448 | tf_op jit(solution)/shard_map/reduce_scatter | solution.py:186
  1483.7 43.2 %all-reduce = (f32[2048]{0:T(1024)}, f32[128]{0:T(128)}, f32[128]{0:T(128)}, f32[2048]{0:T(1024)}) all-reduce(f32[2048]{0:T(1024)S(1)} %dynamic_update_slice.38, f32[128]{0:T(128)S(1)} %bitcast_reduce_fusion, f32[128]{0:T(128)S(1)} %get-tuple-element.21, ...), channel_id=1, replica_groups=mesh['gx'=8,'gy'=4] {'gx','gy'}, use_global_device_ids=true, to_apply=%region_16.17 | all-reduce | flops 4352 | bytes 34816 | tf_op jit(solution)/shard_map/psum | solution.py:257
  1526.9 6.4 psum.51
  1533.3 70.3 %reduce-scatter.26.cloned.1.call-done = bf16[1536,256]{1,0:T(8,128)(2,1)} async-done(((bf16[1536,2048]{1,0:T(8,128)(2,1)}), bf16[1536,256]{1,0:T(8,128)(2,1)}) %reduce-scatter.26.cloned.1.call-update) | async-done | bytes 786448 | tf_op jit(solution)/shard_map/reduce_scatter | solution.py:189
  (266 shorter events, 170.7 us)
Async XLA Ops:
  7.2 44.0 %copy-start.53 = (f32[2048]{0:T(1024)S(1)}, f32[2048]{0:T(1024)}, u32[]{:S(2)}) copy-start(f32[2048]{0:T(1024)} %param.14) | copy-start | bytes 24580
  7.2 39.6 %all-gather.9.cloned.1.call-start = ((), (), s32[]{:S(2)}) async-start(), calls=%async_computation.9 | async-start | bytes 5242880 | tf_op jit(solution)/shard_map/all_gather | solution.py:105
  7.9 90.1 %all-gather.15.cloned.1.call-start = ((), (), s32[]{:S(2)}) async-start(), calls=%async_computation.12 | async-start | bytes 2359296 | tf_op jit(solution)/shard_map/all_gather | solution.py:112
  8.7 130.3 %all-gather.13.cloned.1.call-start = ((), (), s32[]{:S(2)}) async-start(), calls=%async_computation.11 | async-start | bytes 1179648 | tf_op jit(solution)/shard_map/all_gather | solution.py:113
  9.4 170.6 %all-gather.11.cloned.1.call-start = ((), (), s32[]{:S(2)}) async-start(), calls=%async_computation.10 | async-start | bytes 1179648 | tf_op jit(solution)/shard_map/all_gather | solution.py:114
  10.0 221.0 %all-gather.17.cloned.1.call-start = ((), (), s32[]{:S(2)}) async-start(), calls=%async_computation.13 | async-start | bytes 2359296 | tf_op jit(solution)/shard_map/all_gather | solution.py:115
  10.6 379.2 %all-reduce.4.cloned.1.call-start = ((), (), s32[]{:S(2)}) async-start(), calls=%async_computation.14 | async-start | bytes 16777216 | tf_op jit(solution)/shard_map/psum | solution.py:143
  103.3 5.8 copy-start.4
  144.9 41.2 %copy-start.45 = (f32[1024,4]{0,1:T(4,128)}, f32[1024,4]{0,1:T(4,128)S(1)}, u32[]{:S(2)}) copy-start(f32[1024,4]{0,1:T(4,128)S(1)} %get-tuple-element.45) | copy-start | bytes 49156
  145.0 39.7 %copy-start.56 = (f32[128]{0:T(128)S(1)}, f32[128]{0:T(128)}, u32[]{:S(2)}) copy-start(f32[128]{0:T(128)} %param.16) | copy-start | bytes 1540
  196.1 42.4 %copy-start.20 = (bf16[2,2,128,2,512]{4,2,3,1,0:T(8,128)(2,1)}, bf16[2,2,128,2,512]{4,2,3,1,0:T(8,128)(2,1)S(1)}, u32[]{:S(2)}) copy-start(bf16[2,2,128,2,512]{4,2,3,1,0:T(8,128)(2,1)S(1)} %convolution_convert_fusion.8) | copy-start | bytes 3145732
  238.6 252.3 %all-gather.19.cloned.1.call-start = ((), (), s32[]{:S(2)}) async-start(), calls=%async_computation.15 | async-start | bytes 7077888 | tf_op jit(solution)/shard_map/all_gather | solution.py:149
  239.3 285.7 %all-gather.23.cloned.1.call-start = ((), (), s32[]{:S(2)}) async-start(), calls=%async_computation.18 | async-start | bytes 5242880 | tf_op jit(solution)/shard_map/all_gather | solution.py:106
  240.1 386.6 %all-gather.21.cloned.1.call-start = ((), (), s32[]{:S(2)}) async-start(), calls=%async_computation.16 | async-start | bytes 7077888 | tf_op jit(solution)/shard_map/all_gather | solution.py:150
  240.8 583.4 %all-reduce.6.cloned.1.call-start = ((), (), s32[]{:S(2)}) async-start(), calls=%async_computation.19 | async-start | bytes 16777216 | tf_op jit(solution)/shard_map/psum | solution.py:170
  240.9 35.3 %collective-permute-start = (bf16[256,1536]{1,0:T(8,128)(2,1)S(1)}, bf16[256,1536]{1,0:T(8,128)(2,1)S(1)}, u32[]{:S(2)}, u32[]{:S(2)}) collective-permute-start(bf16[256,1536]{1,0:T(8,128)(2,1)S(1)} %copy-done.41), channel_id=1, source_target_pairs={{0,4},{4,8},{8,12},{12,16},{16,20},{20,24},{24,28},{28,0},{1,5},{5... | collective-permute-start | bytes 2359304 | tf_op jit(solution)/shard_map/ppermute | solution.py:24
  242.4 36.2 %collective-permute-start.1 = (bf16[256,1536]{1,0:T(8,128)(2,1)S(1)}, bf16[256,1536]{1,0:T(8,128)(2,1)}, u32[]{:S(2)}, u32[]{:S(2)}) collective-permute-start(bf16[256,1536]{1,0:T(8,128)(2,1)S(1)} %copy-done.41), channel_id=1, source_target_pairs={{0,28},{4,0},{8,4},{12,8},{16,12},{20,16},{24,20},{28,24},{1,29},{... | collective-permute-start | bytes 2359304 | tf_op jit(solution)/shard_map/ppermute | solution.py:27
  276.1 35.5 %collective-permute-start.2 = (bf16[256,1536]{1,0:T(8,128)(2,1)S(1)}, bf16[256,1536]{1,0:T(8,128)(2,1)}, u32[]{:S(2)}, u32[]{:S(2)}) collective-permute-start(bf16[256,1536]{1,0:T(8,128)(2,1)S(1)} %collective-permute-done), channel_id=1, source_target_pairs={{0,4},{4,8},{8,12},{12,16},{16,20},{20,24},{24,28},{28,0},{1,5},{5... | collective-permute-start | bytes 2359304 | tf_op jit(solution)/shard_map/ppermute | solution.py:24
  278.6 40.5 %collective-permute-start.3 = (bf16[256,1536]{1,0:T(8,128)(2,1)}, bf16[256,1536]{1,0:T(8,128)(2,1)}, u32[]{:S(2)}, u32[]{:S(2)}) collective-permute-start(bf16[256,1536]{1,0:T(8,128)(2,1)} %collective-permute-done.1), channel_id=1, source_target_pairs={{0,28},{4,0},{8,4},{12,8},{16,12},{20,16},{24,20},{28,24},{1,29},{... | collective-permute-start | bytes 2359304 | tf_op jit(solution)/shard_map/ppermute | solution.py:27
  311.6 35.1 %collective-permute-start.4 = (bf16[256,1536]{1,0:T(8,128)(2,1)}, bf16[256,1536]{1,0:T(8,128)(2,1)}, u32[]{:S(2)}, u32[]{:S(2)}) collective-permute-start(bf16[256,1536]{1,0:T(8,128)(2,1)} %collective-permute-done.2), channel_id=1, source_target_pairs={{0,4},{4,8},{8,12},{12,16},{16,20},{20,24},{24,28},{28,0},{1,5},{5... | collective-permute-start | bytes 2359304 | tf_op jit(solution)/shard_map/ppermute | solution.py:24
  319.2 36.4 %collective-permute-start.5 = (bf16[256,1536]{1,0:T(8,128)(2,1)}, bf16[256,1536]{1,0:T(8,128)(2,1)S(1)}, u32[]{:S(2)}, u32[]{:S(2)}) collective-permute-start(bf16[256,1536]{1,0:T(8,128)(2,1)} %collective-permute-done.3), channel_id=1, source_target_pairs={{0,28},{4,0},{8,4},{12,8},{16,12},{20,16},{24,20},{28,24},{1,29},{... | collective-permute-start | bytes 2359304 | tf_op jit(solution)/shard_map/ppermute | solution.py:27
  346.7 19.8 %collective-permute-start.6 = (bf16[256,1536]{1,0:T(8,128)(2,1)}, bf16[256,1536]{1,0:T(8,128)(2,1)S(1)}, u32[]{:S(2)}, u32[]{:S(2)}) collective-permute-start(bf16[256,1536]{1,0:T(8,128)(2,1)} %collective-permute-done.4), channel_id=1, source_target_pairs={{0,4},{4,8},{8,12},{12,16},{16,20},{20,24},{24,28},{28,0},{1,5},{5... | collective-permute-start | bytes 2359304 | tf_op jit(solution)/shard_map/ppermute | solution.py:24
  367.5 31.3 %copy-start.47 = (f32[2048]{0:T(1024)S(1)}, f32[2048]{0:T(1024)}, u32[]{:S(2)}) copy-start(f32[2048]{0:T(1024)} %param.21) | copy-start | bytes 24580
  626.6 11.9 copy-start.19
  626.6 27.8 %slice-start = ((s8[6291456]{0:T(1024)(128)(4,1)}), s8[4194304]{0:T(1024)(128)(4,1)S(1)}, s32[]{:S(2)}) async-start(s8[6291456]{0:T(1024)(128)(4,1)} %bitcast.219), calls=%async_computation.28 | async-start | bytes 8388608
  638.5 15.9 slice-start.1
  654.4 6.7 copy-start.58
  673.0 318.6 %reduce-scatter.18.cloned.1.call-start = ((), (), s32[]{:S(2)}) async-start(), calls=%async_computation.23 | async-start | bytes 1179648 | tf_op jit(solution)/shard_map/reduce_scatter | solution.py:241
  824.2 8.2 copy-start.3
  824.2 9.4 copy-start.18
  859.1 6.2 copy-start.21
  872.0 7.0 copy-start.11
  872.0 131.5 %reduce-scatter.16.cloned.1.call-start = ((), (), s32[]{:S(2)}) async-start(), calls=%async_computation.22 | async-start | bytes 1179648 | tf_op jit(solution)/shard_map/reduce_scatter | solution.py:238
  872.4 6.6 copy-start.15
  888.0 161.5 %reduce-scatter.10.cloned.1.call-start = ((), (), s32[]{:S(2)}) async-start(), calls=%async_computation.17 | async-start | bytes 5242880 | tf_op jit(solution)/shard_map/reduce_scatter | solution.py:156
  899.0 8.6 copy-start.30
  899.0 222.8 %reduce-scatter.20.cloned.1.call-start = ((), (), s32[]{:S(2)}) async-start(), calls=%async_computation.24 | async-start | bytes 2359296 | tf_op jit(solution)/shard_map/reduce_scatter | solution.py:244
  907.4 285.8 %reduce-scatter.14.cloned.1.call-start = ((), (), s32[]{:S(2)}) async-start(), calls=%async_computation.21 | async-start | bytes 2359296 | tf_op jit(solution)/shard_map/reduce_scatter | solution.py:235
  915.1 7.6 copy-start.28
  936.8 5.2 copy-start.48
  948.0 291.0 %reduce-scatter.12.cloned.1.call-start = ((), (), s32[]{:S(2)}) async-start(), calls=%async_computation.20 | async-start | bytes 5242880 | tf_op jit(solution)/shard_map/reduce_scatter | solution.py:231
  955.8 404.7 %reduce-scatter.22.cloned.1.call-start = ((), (), s32[]{:S(2)}) async-start(), calls=%async_computation.25 | async-start | bytes 7077888 | tf_op jit(solution)/shard_map/reduce_scatter | solution.py:183
  967.4 513.9 %reduce-scatter.24.cloned.1.call-start = ((), (), s32[]{:S(2)}) async-start(), calls=%async_computation.26 | async-start | bytes 7077888 | tf_op jit(solution)/shard_map/reduce_scatter | solution.py:186
  979.2 624.4 %reduce-scatter.26.cloned.1.call-start = ((), (), s32[]{:S(2)}) async-start(), calls=%async_computation.27 | async-start | bytes 7077888 | tf_op jit(solution)/shard_map/reduce_scatter | solution.py:189
  990.6 248.5 %copy-start.9 = (bf16[1024,512]{1,0:T(8,128)(2,1)S(1)}, bf16[1024,512]{1,0:T(8,128)(2,1)}, u32[]{:S(2)}) copy-start(bf16[1024,512]{1,0:T(8,128)(2,1)} %param.13) | copy-start | bytes 3145732
  990.6 248.4 %copy-start.50 = (f32[1024]{0:T(1024)S(1)}, f32[1024]{0:T(1024)}, u32[]{:S(2)}) copy-start(f32[1024]{0:T(1024)} %copy-done.49) | copy-start | bytes 12292
  1195.1 410.9 %copy-start.52 = (f32[1024]{0:T(1024)S(1)}, f32[1024]{0:T(1024)}, u32[]{:S(2)}) copy-start(f32[1024]{0:T(1024)} %get-tuple-element.48) | copy-start | bytes 12292
  1239.0 366.9 %copy-start.26 = (bf16[1024,512]{1,0:T(8,128)(2,1)S(1)}, bf16[1024,512]{1,0:T(8,128)(2,1)}, u32[]{:S(2)}) copy-start(bf16[1024,512]{1,0:T(8,128)(2,1)} %reduce-scatter.12.cloned.1.call-done) | copy-start | bytes 3145732
  (40 other events, 99.9 us)
Sparse Core Ops, SparseCore 0:
  9.6 37.1 all-gather.8
  48.9 49.0 all-gather.14
  100.1 38.7 all-gather.12
  141.0 38.9 all-gather.10
  181.9 49.0 all-gather.16
  238.7 151.0 all-reduce.3
  392.0 98.8 all-gather.18
  492.4 32.6 all-gather.22
  527.1 99.4 all-gather.20
  673.1 151.0 all-reduce.5
  872.1 64.3 reduce-scatter.17
  940.4 63.1 reduce-scatter.15
  1006.0 43.4 reduce-scatter.9
  1052.9 68.9 reduce-scatter.19
  1125.8 67.3 reduce-scatter.13
  1195.6 43.3 reduce-scatter.11
  1242.5 117.9 reduce-scatter.21
  1363.9 117.2 reduce-scatter.23
  1484.8 118.7 reduce-scatter.25
